TPU v7x, 256 devices: a whole 4x4x8 slice. The times are simulated.
256 devices in a mesh: rep: 16 (over z, core), rows: 16 (over y, x).
Axes of the slice: x: 4, y: 4, z: 8, core: 2. Of those that a mesh axis runs over, the one named last changes fastest.
Arguments:
- weights: bfloat16 [7168, 2048], P('rows'), may hold values from -6 to 6
- momentum: float32 [16, 7168, 2048], P('rep', 'rows'), may hold values from -8 to 8
- gradient: bfloat16 [16, 7168, 2048], P('rep', 'rows'), may hold values from -8 to 8
- right_factor: float32 [2048, 512], P('rows'), may hold values from -6 to 6
Outputs:
- new_weights: bfloat16 [7168, 2048], P('rows')
- new_momentum: float32 [16, 7168, 2048], P('rep', 'rows')
- new_right: float32 [2048, 512], P('rows')
All inputs are finite; a program needn't handle non-finite values.
Results may differ from a plain program's by a relative error of at most 0.019.
Values may be sent and summed in bfloat16 or wider, within the bound.
No kernel may reach another device: no remote copies, remote signals or barrier semaphores. Data moves between devices by JAX's collectives and lax.ppermute only.
A program may use at most 64 MiB of HBM per device.

v0:
```python
import jax
import jax.numpy as jnp
from jax import lax
from jax.sharding import Mesh
from jax.sharding import PartitionSpec as P

M = 7168
N = 2048
ROWS = ("rows_0", "rows_1")
momentum_keep = 0.05
learn_rate = 0.5
tiny = 1e-06


def from_everyone(value, axis):
    size = lax.axis_size(axis)
    return lax.all_to_all(
        jnp.broadcast_to(value[None], (size, *value.shape)), axis, 0, 0, tiled=True
    )


def laid_out(blocks, dim):
    dims = list(blocks.shape[1:])
    dims[dim] *= blocks.shape[0]
    return jnp.moveaxis(blocks, 0, dim).reshape(dims)


def gather_directly(value, axis, dim):
    blocks = from_everyone(value, axis)
    return laid_out(blocks, dim)


def gathered_total(value, axis):
    return lax.all_gather(value, axis).astype(jnp.float32).sum(0)


def sum_by_axis(terms, axes):
    running = terms.astype(jnp.bfloat16)
    for axis in axes:
        running = lax.psum_scatter(running, axis, scatter_dimension=0, tiled=True)
    return running.astype(jnp.float32)


def over_axes(value, axes):
    for axis in axes:
        value = lax.psum(value, axis)
    return value


def per_device(weights, momentum, gradient, right_factor):
    groups = lax.axis_size("rep")
    combined = momentum[0] + gradient[0].astype(jnp.float32)
    combined_half = combined.astype(jnp.bfloat16)
    columns = combined.shape[1]
    block = combined_half
    left_local = jnp.dot(
        block,
        gather_directly(right_factor.astype(jnp.bfloat16), ROWS, 0),
        preferred_element_type=jnp.float32,
    )
    left_local = lax.optimization_barrier(left_local.astype(jnp.bfloat16)).astype(jnp.float32)
    left_mean = gathered_total(left_local.astype(jnp.bfloat16), "rep").astype(jnp.float32) / groups
    gram = lax.psum(jnp.dot(left_mean.T, left_mean, precision=lax.Precision.HIGHEST), ROWS)
    chol = jnp.linalg.cholesky(gram)
    left_orth = jax.scipy.linalg.solve_triangular(chol, left_mean.T, lower=True).T
    left_half = left_orth.astype(jnp.bfloat16)
    block = combined_half
    right_part = sum_by_axis(
        jnp.einsum("ij,ik->jk", block, left_half, preferred_element_type=jnp.float32), ROWS
    )
    right_mean = gathered_total(right_part.astype(jnp.bfloat16), "rep").astype(jnp.float32) / groups
    squares = over_axes(jnp.sum(right_mean * right_mean, axis=0), ROWS)
    new_right = right_mean / jnp.sqrt(squares / columns + tiny)
    stacked = jnp.stack([right_mean.astype(jnp.bfloat16), new_right.astype(jnp.bfloat16)], 0)
    both = jnp.einsum(
        "ir,skr->sik",
        left_half,
        lax.all_gather(stacked, ROWS, axis=1, tiled=True),
        preferred_element_type=jnp.float32,
    )
    feedback = both[0]
    update = both[1]
    new_momentum = combined - momentum_keep * feedback
    new_weights = (weights.astype(jnp.float32) - learn_rate * jnp.sqrt(M / N) * update).astype(
        jnp.bfloat16
    )
    return (new_weights, new_momentum[None], new_right)


def solution(mesh):
    split = Mesh(mesh.devices.reshape(mesh.shape["rep"], 4, 4), ("rep", "rows_0", "rows_1"))
    in_specs = (P(ROWS, None), P("rep", ROWS, None), P("rep", ROWS, None), P(ROWS, None))
    out_specs = (P(ROWS, None), P("rep", ROWS, None), P(ROWS, None))
    return jax.shard_map(
        per_device, mesh=split, in_specs=in_specs, out_specs=out_specs, check_vma=False
    )
```

profile of v0, /device:TPU:1, one launch (start us, length us, event | category | flops | bytes accessed | tf_op | source)
XLA Modules:
  0.0 543.4 jit_solution(8520991013041620438)
XLA Ops:
  7.2 1.1 convert_element_type.64
  8.4 0.2 broadcast_in_dim.3
  8.6 34.8 %all_to_all.5 = bf16[16,128,512]{2,1,0:T(8,128)(2,1)S(1)} all-to-all(bf16[16,128,512]{2,1,0:T(8,128)(2,1)S(1)} %broadcast_in_dim.3), channel_id=1, replica_groups=mesh['rep'=16,'rows_0'=4,'rows_1'=4] {'rows_0','rows_1'}, dimensions={0} | all-to-all | bytes 4194304 | tf_op jit(solution)/shard_map/all_to_all | solution.py:17
  43.3 1.9 convolution_convert_fusion.1
  45.4 51.9 %all-gather.8.cloned.1.call-done = bf16[7168,512]{1,0:T(8,128)(2,1)} async-done(((bf16[448,512]{1,0:T(8,128)(2,1)}), bf16[7168,512]{1,0:T(8,128)(2,1)}) %all-gather.8.cloned.1.call-update) | async-done | bytes 7340048 | tf_op jit(solution)/shard_map/all_gather | solution.py:34
  97.2 4.2 convert_reduce_fusion
  101.4 2.9 fusion.7
  104.4 0.5 reduce-scatter.3.cloned.1.call-start
  104.9 1.0 multiply_bitcast_fusion
  105.9 92.8 %all-reduce.3.cloned.1.call-done = f32[512,512]{0,1:T(8,128)} async-done(((f32[512,512]{0,1:T(8,128)}), f32[512,512]{0,1:T(8,128)}) %all-reduce.3.cloned.1.call-update) | async-done | bytes 1048592 | tf_op jit(solution)/shard_map/psum | solution.py:63
  198.7 1.6 copy.8
  200.3 1.4 fusion.6
  201.8 1.0 copy-done.4
  202.7 11.7 %cholesky.104 = f32[128,128]{1,0:T(8,128)S(1)} custom-call(f32[128,128]{1,0:T(8,128)S(1)} %cholesky.266), custom_call_target="Cholesky" | custom-call | tf_op jit(solution)/shard_map/jit(cholesky)/cholesky | solution.py:64
  214.5 9.8 %custom-call.31 = f32[1,128,128]{1,2,0:T(8,128)S(1)} custom-call(f32[1,128,128]{2,1,0:T(8,128)S(1)} %get-tuple-element.32), custom_call_target="InvertDiagBlocksLowerTriangular" | custom-call | tf_op jit(solution)/shard_map/jit(cholesky)/cholesky | solution.py:64
  224.3 0.1 cholesky.224
  224.4 1.2 constant_dynamic-update-slice_fusion.3
  225.7 1.3 convolution_subtract_fusion.3
  227.0 11.7 %cholesky.217 = f32[128,128]{1,0:T(8,128)S(1)} custom-call(f32[128,128]{1,0:T(8,128)S(1)} %cholesky.270), custom_call_target="Cholesky" | custom-call | tf_op jit(solution)/shard_map/jit(cholesky)/cholesky | solution.py:64
  238.7 10.0 %custom-call.32 = f32[1,128,128]{1,2,0:T(8,128)S(1)} custom-call(f32[1,128,128]{2,1,0:T(8,128)S(1)} %get-tuple-element.29), custom_call_target="InvertDiagBlocksLowerTriangular" | custom-call | tf_op jit(solution)/shard_map/jit(cholesky)/cholesky | solution.py:64
  248.7 0.3 convolution_dynamic-update-slice_fusion
  248.9 1.3 convolution_subtract_fusion.4
  250.2 11.7 %cholesky.238 = f32[128,128]{1,0:T(8,128)S(1)} custom-call(f32[128,128]{1,0:T(8,128)S(1)} %cholesky.275), custom_call_target="Cholesky" | custom-call | tf_op jit(solution)/shard_map/jit(cholesky)/cholesky | solution.py:64
  262.0 0.7 compare_reduce_fusion.1
  262.7 9.8 %custom-call.33 = f32[1,128,128]{1,2,0:T(8,128)S(1)} custom-call(f32[1,128,128]{2,1,0:T(8,128)S(1)} %get-tuple-element.26), custom_call_target="InvertDiagBlocksLowerTriangular" | custom-call | tf_op jit(solution)/shard_map/jit(cholesky)/cholesky | solution.py:64
  272.5 0.2 convolution_dynamic-update-slice_fusion.1
  272.7 1.2 convolution_subtract_fusion.5
  273.9 11.7 %cholesky.255 = f32[128,128]{1,0:T(8,128)S(1)} custom-call(f32[128,128]{1,0:T(8,128)S(1)} %convolution_subtract_fusion.5), custom_call_target="Cholesky" | custom-call | tf_op jit(solution)/shard_map/jit(cholesky)/cholesky | solution.py:64
  285.7 0.6 compare_reduce_fusion
  286.3 0.9 compare_reduce_fusion.2
  289.7 1.1 select_select_fusion
  290.8 11.7 %while.1 = (s32[]{:T(128)}, f32[512,512]{1,0:T(8,128)}, s32[4,2]{0,1:T(2,128)S(1)}, f32[4,128,128]{2,1,0:T(8,128)S(1)}, s32[]{:T(128)}) while((s32[]{:T(128)}, f32[512,512]{1,0:T(8,128)}, s32[4,2]{0,1:T(2,128)S(1)}, f32[4,128,128]{2,1,0:T(8,128)S(1)}, s32[]{:T(128)}) %tuple.35), condition=%wide.while_cond, body=%wide.while_body.sunk | while | flops 2 | bytes 131189 | solution.py:65
  290.8 0.1 constant_dynamic-slice_fusion.2
  290.9 0.6 fusion.57
  291.5 2.2 bitcast_dynamic-update-slice_fusion.2
  293.8 0.1 constant_dynamic-slice_fusion.2
  293.9 0.6 fusion.57
  294.5 2.2 bitcast_dynamic-update-slice_fusion.2
  296.8 0.6 fusion.57
  297.4 2.2 bitcast_dynamic-update-slice_fusion.2
  299.7 0.1 constant_dynamic-slice_fusion.2
  299.7 0.6 fusion.57
  300.3 2.2 bitcast_dynamic-update-slice_fusion.2
  302.5 39.3 %custom-call.34 = f32[4,128,128]{1,2,0:T(8,128)S(1)} custom-call(f32[4,128,128]{2,1,0:T(8,128)S(1)} %get-tuple-element.10), custom_call_target="InvertDiagBlocksLowerTriangular" | custom-call | tf_op jit(solution)/shard_map/jit(_solve_triangular)/triangular_solve | solution.py:65
  341.9 1.4 fusion.48
  343.3 1.3 convolution_subtract_fusion.2
  344.6 0.3 fusion.47
  345.0 1.5 convolution_subtract_fusion.1
  346.5 0.3 fusion.46
  346.9 1.8 convolution_subtract_fusion
  348.7 0.3 convolution_convert_fusion.2
  349.0 2.7 convolution_convert_fusion
  351.8 33.1 %reduce-scatter.3.cloned.1.call-done = bf16[512,512]{1,0:T(8,128)(2,1)} async-done(((bf16[2048,512]{1,0:T(8,128)(2,1)}), bf16[512,512]{1,0:T(8,128)(2,1)}) %reduce-scatter.3.cloned.1.call-update) | async-done | bytes 524304 | tf_op jit(solution)/shard_map/reduce_scatter | solution.py:40
  385.0 23.9 %reduce-scatter.5.cloned.1.call-done = bf16[128,512]{1,0:T(8,128)(2,1)} async-done(((bf16[512,512]{1,0:T(8,128)(2,1)}), bf16[128,512]{1,0:T(8,128)(2,1)}) %reduce-scatter.5.cloned.1.call-update) | async-done | bytes 131088 | tf_op jit(solution)/shard_map/reduce_scatter | solution.py:40
  409.0 43.6 %all-gather.10.cloned.1.call-done = bf16[2048,512]{1,0:T(8,128)(2,1)} async-done(((bf16[128,512]{1,0:T(8,128)(2,1)}), bf16[2048,512]{1,0:T(8,128)(2,1)}) %all-gather.10.cloned.1.call-update) | async-done | bytes 2097168 | tf_op jit(solution)/shard_map/all_gather | solution.py:34
  452.6 1.9 convert_reduce_fusion.1
  454.6 8.5 %psum.22 = f32[512]{0:T(512)S(1)} all-reduce(f32[512]{0:T(512)S(1)} %multiply_reduce_fusion), channel_id=1, replica_groups=mesh['rep'=16,'rows_0'=4,'rows_1'=4] {'rows_0'}, use_global_device_ids=true, to_apply=%region_14.15 | all-reduce | flops 512 | bytes 4096 | tf_op jit(solution)/shard_map/psum | solution.py:46
  463.0 8.4 %psum.23 = f32[512]{0:T(512)S(1)} all-reduce(f32[512]{0:T(512)S(1)} %psum.22), channel_id=1, replica_groups=mesh['rep'=16,'rows_0'=4,'rows_1'=4] {'rows_1'}, use_global_device_ids=true, to_apply=%region_15.16 | all-reduce | flops 512 | bytes 4096 | tf_op jit(solution)/shard_map/psum | solution.py:46
  471.5 0.7 multiply_divide_fusion
  472.2 0.7 pad_maximum_fusion.1
  473.0 54.2 %all-gather.6.cloned.1.call-done = bf16[2,2048,512]{2,1,0:T(8,128)(2,1)} async-done(((bf16[2,128,512]{2,1,0:T(8,128)(2,1)}), bf16[2,2048,512]{2,1,0:T(8,128)(2,1)}) %all-gather.6.cloned.1.call-update) | async-done | bytes 4194320 | tf_op jit(solution)/shard_map/all_gather | solution.py:78
  527.1 4.4 convolution_bitcast_fusion
  531.6 2.8 fusion
  534.5 1.9 fusion.3
  (36 shorter events, 0.7 us)
Async XLA Ops:
  7.2 36.2 %copy-start.3 = (bf16[1,448,2048]{2,1,0:T(8,128)(2,1)S(1)}, bf16[1,448,2048]{2,1,0:T(8,128)(2,1)}, u32[]{:S(2)}) copy-start(bf16[1,448,2048]{2,1,0:T(8,128)(2,1)} %param.6) | copy-start | bytes 5505028
  7.2 90.1 %all-gather.8.cloned.1.call-start = ((), (), s32[]{:S(2)}) async-start(), calls=%async_computation.7 | async-start | bytes 7798784 | tf_op jit(solution)/shard_map/all_gather | solution.py:34
  7.2 36.1 %copy-start = (f32[1,448,2048]{2,1,0:T(8,128)S(1)}, f32[1,448,2048]{2,1,0:T(8,128)}, u32[]{:S(2)}) copy-start(f32[1,448,2048]{2,1,0:T(8,128)} %param.5) | copy-start | bytes 11010052
  45.3 153.4 %all-reduce.3.cloned.1.call-start = ((), (), s32[]{:S(2)}) async-start(), calls=%async_computation.3 | async-start | bytes 2097152 | tf_op jit(solution)/shard_map/psum | solution.py:63
  104.4 280.5 %reduce-scatter.3.cloned.1.call-start = ((), (), s32[]{:S(2)}) async-start(), calls=%async_computation.4 | async-start | bytes 2621440 | tf_op jit(solution)/shard_map/reduce_scatter | solution.py:40
  201.7 1.0 copy-start.4
  341.9 7.2 %copy-start.1 = (f32[1,448,2048]{2,1,0:T(8,128)S(1)}, f32[1,448,2048]{2,1,0:T(8,128)}, u32[]{:S(2)}) copy-start(f32[1,448,2048]{2,1,0:T(8,128)} %param.5) | copy-start | bytes 11010052
  351.7 57.2 %reduce-scatter.5.cloned.1.call-start = ((), (), s32[]{:S(2)}) async-start(), calls=%async_computation.5 | async-start | bytes 655360 | tf_op jit(solution)/shard_map/reduce_scatter | solution.py:40
  384.9 67.7 %all-gather.10.cloned.1.call-start = ((), (), s32[]{:S(2)}) async-start(), calls=%async_computation.8 | async-start | bytes 2228224 | tf_op jit(solution)/shard_map/all_gather | solution.py:34
  409.0 118.2 %all-gather.6.cloned.1.call-start = ((), (), s32[]{:S(2)}) async-start(), calls=%async_computation.6 | async-start | bytes 4456448 | tf_op jit(solution)/shard_map/all_gather | solution.py:78
  527.1 4.5 copy-start.2
  531.6 2.9 copy-start.5
Sparse Core Ops, SparseCore 0:
  45.4 51.7 all-gather.7
  104.5 94.1 all-reduce.2
  351.9 33.0 reduce-scatter.2
  387.3 21.5 reduce-scatter.4
  410.6 41.9 all-gather.9
  473.1 53.9 all-gather.5
where the time goes:
time: 548 us; the launch traced here: 543 us
  waiting for transfers between devices  300 us (55%)
  other arithmetic  135 us (25%)
  blocking collectives  51.6 us (9%)
  matrix products  24.6 us (4%)
  between operations  17.2 us (3%)
  local copies, waits for them, and re-layouts  14.5 us (3%)
    all_gather x2, waiting for transfers between devices, gathered_total(): return lax.all_gather(value, axis).astype(jnp.float32).sum(0)  95.5 us
    psum x1, waiting for transfers between devices, per_device(): lax.psum(jnp.dot(left_mean.T, left_mean, precision=lax.Precision.HIGHEST)...  92.8 us
    another operation x14, other arithmetic, per_device(): chol = jnp.linalg.cholesky(gram)  78.8 us
    reduce_scatter x2, waiting for transfers between devices, sum_by_axis(): running = lax.psum_scatter(running, axis, scatter_dimension=0, tiled=True)  57.1 us
    all_gather x1, waiting for transfers between devices, per_device(): lax.all_gather(stacked, ROWS, axis=1, tiled=True)  54.2 us
    another operation x3, other arithmetic, per_device(): jax.scipy.linalg.solve_triangular(chol, left_mean.T, lower=True)  40.4 us
    all_to_all x1, blocking collectives, from_everyone(): lax.all_to_all(jnp.broadcast_to(value[None], (size, *value.shape)), axis,...  34.8 us
    psum x2, blocking collectives, over_axes(): value = lax.psum(value, axis)  16.8 us
  transfers between devices with their start and end apart: 6, of which 6 were waited for; matrix products, arithmetic and copies ran while one was open for 0% of the time, Pallas kernels for 0%

commit v1 on v0

--- a/solution.py
+++ b/solution.py
@@ -3,6 +3,7 @@
 from jax import lax
 from jax.sharding import Mesh
 from jax.sharding import PartitionSpec as P
+from jax.lax import all_gather
 
 M = 7168
 N = 2048
@@ -72,11 +73,9 @@
     squares = over_axes(jnp.sum(right_mean * right_mean, axis=0), ROWS)
     new_right = right_mean / jnp.sqrt(squares / columns + tiny)
     stacked = jnp.stack([right_mean.astype(jnp.bfloat16), new_right.astype(jnp.bfloat16)], 0)
+    push_tasks = lambda x_in: jnp.concatenate(all_gather(x_in, ROWS), 1)
     both = jnp.einsum(
-        "ir,skr->sik",
-        left_half,
-        lax.all_gather(stacked, ROWS, axis=1, tiled=True),
-        preferred_element_type=jnp.float32,
+        "ir,skr->sik", left_half, push_tasks(stacked), preferred_element_type=jnp.float32
     )
     feedback = both[0]
     update = both[1]

time: 548 us -> 548 us (level)
  no operation moved by 1% of the time
where the time goes in v1:
time: 548 us; the launch traced here: 544 us
  waiting for transfers between devices  300 us (55%)
  other arithmetic  135 us (25%)
  blocking collectives  51.6 us (9%)
  matrix products  22.3 us (4%)
  between operations  17.2 us (3%)
  local copies, waits for them, and re-layouts  17 us (3%)
    all_gather x2, waiting for transfers between devices, gathered_total(): return lax.all_gather(value, axis).astype(jnp.float32).sum(0)  95.5 us
    psum x1, waiting for transfers between devices, per_device(): lax.psum(jnp.dot(left_mean.T, left_mean, precision=lax.Precision.HIGHEST)...  92.8 us
    another operation x14, other arithmetic, per_device(): chol = jnp.linalg.cholesky(gram)  78.8 us
    reduce_scatter x2, waiting for transfers between devices, sum_by_axis(): running = lax.psum_scatter(running, axis, scatter_dimension=0, tiled=True)  57.1 us
    all_gather x1, waiting for transfers between devices, per_device(): push_tasks = lambda x_in: jnp.concatenate(all_gather(x_in, ROWS), 1)  54.1 us
    another operation x3, other arithmetic, per_device(): jax.scipy.linalg.solve_triangular(chol, left_mean.T, lower=True)  40.4 us
    all_to_all x1, blocking collectives, from_everyone(): lax.all_to_all(jnp.broadcast_to(value[None], (size, *value.shape)), axis,...  34.8 us
    psum x2, blocking collectives, over_axes(): value = lax.psum(value, axis)  16.8 us
  transfers between devices with their start and end apart: 6, of which 6 were waited for; matrix products, arithmetic and copies ran while one was open for 0% of the time, Pallas kernels for 0%

profile of v1, /device:TPU:1, one launch (start us, length us, event | category | flops | bytes accessed | tf_op | source)
XLA Modules:
  0.0 543.6 jit_solution(10056313816332258750)
XLA Ops:
  7.2 1.1 convert_element_type.64
  8.4 0.2 broadcast_in_dim.3
  8.6 34.8 %all_to_all.5 = bf16[16,128,512]{2,1,0:T(8,128)(2,1)S(1)} all-to-all(bf16[16,128,512]{2,1,0:T(8,128)(2,1)S(1)} %broadcast_in_dim.3), channel_id=1, replica_groups=mesh['rep'=16,'rows_0'=4,'rows_1'=4] {'rows_0','rows_1'}, dimensions={0} | all-to-all | bytes 4194304 | tf_op jit(solution)/shard_map/all_to_all | solution.py:18
  43.3 1.9 convolution_convert_fusion.1
  45.4 51.9 %all-gather.7.cloned.1.call-done = bf16[7168,512]{1,0:T(8,128)(2,1)} async-done(((bf16[448,512]{1,0:T(8,128)(2,1)}), bf16[7168,512]{1,0:T(8,128)(2,1)}) %all-gather.7.cloned.1.call-update) | async-done | bytes 7340048 | tf_op jit(solution)/shard_map/all_gather | solution.py:35
  97.2 4.2 convert_reduce_fusion
  101.4 2.9 fusion.7
  104.4 0.5 reduce-scatter.3.cloned.1.call-start
  104.9 1.0 multiply_bitcast_fusion
  105.9 92.8 %all-reduce.3.cloned.1.call-done = f32[512,512]{0,1:T(8,128)} async-done(((f32[512,512]{0,1:T(8,128)}), f32[512,512]{0,1:T(8,128)}) %all-reduce.3.cloned.1.call-update) | async-done | bytes 1048592 | tf_op jit(solution)/shard_map/psum | solution.py:64
  198.7 1.6 copy.11
  200.3 1.4 fusion.6
  201.8 1.0 copy-done.4
  202.7 11.7 %cholesky.104 = f32[128,128]{1,0:T(8,128)S(1)} custom-call(f32[128,128]{1,0:T(8,128)S(1)} %cholesky.266), custom_call_target="Cholesky" | custom-call | tf_op jit(solution)/shard_map/jit(cholesky)/cholesky | solution.py:65
  214.5 9.8 %custom-call.31 = f32[1,128,128]{1,2,0:T(8,128)S(1)} custom-call(f32[1,128,128]{2,1,0:T(8,128)S(1)} %get-tuple-element.32), custom_call_target="InvertDiagBlocksLowerTriangular" | custom-call | tf_op jit(solution)/shard_map/jit(cholesky)/cholesky | solution.py:65
  224.3 0.1 cholesky.224
  224.4 1.2 constant_dynamic-update-slice_fusion.3
  225.7 1.3 convolution_subtract_fusion.3
  227.0 11.7 %cholesky.217 = f32[128,128]{1,0:T(8,128)S(1)} custom-call(f32[128,128]{1,0:T(8,128)S(1)} %cholesky.270), custom_call_target="Cholesky" | custom-call | tf_op jit(solution)/shard_map/jit(cholesky)/cholesky | solution.py:65
  238.7 10.0 %custom-call.32 = f32[1,128,128]{1,2,0:T(8,128)S(1)} custom-call(f32[1,128,128]{2,1,0:T(8,128)S(1)} %get-tuple-element.29), custom_call_target="InvertDiagBlocksLowerTriangular" | custom-call | tf_op jit(solution)/shard_map/jit(cholesky)/cholesky | solution.py:65
  248.7 0.3 convolution_dynamic-update-slice_fusion
  248.9 1.3 convolution_subtract_fusion.4
  250.2 11.7 %cholesky.238 = f32[128,128]{1,0:T(8,128)S(1)} custom-call(f32[128,128]{1,0:T(8,128)S(1)} %cholesky.275), custom_call_target="Cholesky" | custom-call | tf_op jit(solution)/shard_map/jit(cholesky)/cholesky | solution.py:65
  262.0 0.7 compare_reduce_fusion.1
  262.7 9.8 %custom-call.33 = f32[1,128,128]{1,2,0:T(8,128)S(1)} custom-call(f32[1,128,128]{2,1,0:T(8,128)S(1)} %get-tuple-element.26), custom_call_target="InvertDiagBlocksLowerTriangular" | custom-call | tf_op jit(solution)/shard_map/jit(cholesky)/cholesky | solution.py:65
  272.5 0.2 convolution_dynamic-update-slice_fusion.1
  272.7 1.2 convolution_subtract_fusion.5
  273.9 11.7 %cholesky.255 = f32[128,128]{1,0:T(8,128)S(1)} custom-call(f32[128,128]{1,0:T(8,128)S(1)} %convolution_subtract_fusion.5), custom_call_target="Cholesky" | custom-call | tf_op jit(solution)/shard_map/jit(cholesky)/cholesky | solution.py:65
  285.7 0.6 compare_reduce_fusion
  286.3 0.9 compare_reduce_fusion.2
  289.7 1.1 select_select_fusion
  290.8 11.7 %while.1 = (s32[]{:T(128)}, f32[512,512]{1,0:T(8,128)}, s32[4,2]{0,1:T(2,128)S(1)}, f32[4,128,128]{2,1,0:T(8,128)S(1)}, s32[]{:T(128)}) while((s32[]{:T(128)}, f32[512,512]{1,0:T(8,128)}, s32[4,2]{0,1:T(2,128)S(1)}, f32[4,128,128]{2,1,0:T(8,128)S(1)}, s32[]{:T(128)}) %tuple.35), condition=%wide.while_cond, body=%wide.while_body.sunk | while | flops 2 | bytes 131189 | solution.py:66
  290.8 0.1 constant_dynamic-slice_fusion.2
  290.9 0.6 fusion.57
  291.5 2.2 bitcast_dynamic-update-slice_fusion.2
  293.9 0.6 fusion.57
  294.5 2.2 bitcast_dynamic-update-slice_fusion.2
  296.8 0.6 fusion.57
  297.4 2.2 bitcast_dynamic-update-slice_fusion.2
  299.7 0.1 constant_dynamic-slice_fusion.2
  299.7 0.6 fusion.57
  300.3 2.2 bitcast_dynamic-update-slice_fusion.2
  302.5 39.3 %custom-call.34 = f32[4,128,128]{1,2,0:T(8,128)S(1)} custom-call(f32[4,128,128]{2,1,0:T(8,128)S(1)} %get-tuple-element.10), custom_call_target="InvertDiagBlocksLowerTriangular" | custom-call | tf_op jit(solution)/shard_map/jit(_solve_triangular)/triangular_solve | solution.py:66
  341.9 1.4 fusion.48
  343.3 1.3 convolution_subtract_fusion.2
  344.6 0.3 fusion.47
  345.0 1.5 convolution_subtract_fusion.1
  346.5 0.3 fusion.46
  346.9 1.8 convolution_subtract_fusion
  348.7 0.3 convolution_convert_fusion.2
  349.0 2.7 convolution_convert_fusion
  351.8 33.1 %reduce-scatter.3.cloned.1.call-done = bf16[512,512]{1,0:T(8,128)(2,1)} async-done(((bf16[2048,512]{1,0:T(8,128)(2,1)}), bf16[512,512]{1,0:T(8,128)(2,1)}) %reduce-scatter.3.cloned.1.call-update) | async-done | bytes 524304 | tf_op jit(solution)/shard_map/reduce_scatter | solution.py:41
  385.0 23.9 %reduce-scatter.5.cloned.1.call-done = bf16[128,512]{1,0:T(8,128)(2,1)} async-done(((bf16[512,512]{1,0:T(8,128)(2,1)}), bf16[128,512]{1,0:T(8,128)(2,1)}) %reduce-scatter.5.cloned.1.call-update) | async-done | bytes 131088 | tf_op jit(solution)/shard_map/reduce_scatter | solution.py:41
  409.0 43.6 %all-gather.9.cloned.1.call-done = bf16[2048,512]{1,0:T(8,128)(2,1)} async-done(((bf16[128,512]{1,0:T(8,128)(2,1)}), bf16[2048,512]{1,0:T(8,128)(2,1)}) %all-gather.9.cloned.1.call-update) | async-done | bytes 2097168 | tf_op jit(solution)/shard_map/all_gather | solution.py:35
  452.6 1.9 convert_reduce_fusion.1
  454.6 8.5 %psum.22 = f32[512]{0:T(512)S(1)} all-reduce(f32[512]{0:T(512)S(1)} %multiply_reduce_fusion), channel_id=1, replica_groups=mesh['rep'=16,'rows_0'=4,'rows_1'=4] {'rows_0'}, use_global_device_ids=true, to_apply=%region_14.15 | all-reduce | flops 512 | bytes 4096 | tf_op jit(solution)/shard_map/psum | solution.py:47
  463.0 8.4 %psum.23 = f32[512]{0:T(512)S(1)} all-reduce(f32[512]{0:T(512)S(1)} %psum.22), channel_id=1, replica_groups=mesh['rep'=16,'rows_0'=4,'rows_1'=4] {'rows_1'}, use_global_device_ids=true, to_apply=%region_15.16 | all-reduce | flops 512 | bytes 4096 | tf_op jit(solution)/shard_map/psum | solution.py:47
  471.5 0.7 multiply_divide_fusion
  472.2 0.7 pad_maximum_fusion.1
  473.0 54.1 %all-gather.11.cloned.1.call-done = bf16[32,128,512]{2,1,0:T(8,128)(2,1)} async-done(((bf16[2,128,512]{2,1,0:T(8,128)(2,1)}), bf16[32,128,512]{2,1,0:T(8,128)(2,1)}) %all-gather.11.cloned.1.call-update) | async-done | bytes 4194320 | tf_op jit(solution)/shard_map/all_gather | solution.py:76
  527.1 2.5 copy.12
  529.6 2.2 convolution_bitcast_fusion
  531.8 2.9 fusion
  534.6 1.9 fusion.3
  (37 shorter events, 0.7 us)
Async XLA Ops:
  7.2 36.2 %copy-start.3 = (bf16[1,448,2048]{2,1,0:T(8,128)(2,1)S(1)}, bf16[1,448,2048]{2,1,0:T(8,128)(2,1)}, u32[]{:S(2)}) copy-start(bf16[1,448,2048]{2,1,0:T(8,128)(2,1)} %param.6) | copy-start | bytes 5505028
  7.2 90.1 %all-gather.7.cloned.1.call-start = ((), (), s32[]{:S(2)}) async-start(), calls=%async_computation.6 | async-start | bytes 7798784 | tf_op jit(solution)/shard_map/all_gather | solution.py:35
  7.2 36.1 %copy-start = (f32[1,448,2048]{2,1,0:T(8,128)S(1)}, f32[1,448,2048]{2,1,0:T(8,128)}, u32[]{:S(2)}) copy-start(f32[1,448,2048]{2,1,0:T(8,128)} %param.5) | copy-start | bytes 11010052
  45.3 153.4 %all-reduce.3.cloned.1.call-start = ((), (), s32[]{:S(2)}) async-start(), calls=%async_computation.3 | async-start | bytes 2097152 | tf_op jit(solution)/shard_map/psum | solution.py:64
  104.4 280.5 %reduce-scatter.3.cloned.1.call-start = ((), (), s32[]{:S(2)}) async-start(), calls=%async_computation.4 | async-start | bytes 2621440 | tf_op jit(solution)/shard_map/reduce_scatter | solution.py:41
  201.7 1.0 copy-start.4
  341.9 7.2 %copy-start.1 = (f32[1,448,2048]{2,1,0:T(8,128)S(1)}, f32[1,448,2048]{2,1,0:T(8,128)}, u32[]{:S(2)}) copy-start(f32[1,448,2048]{2,1,0:T(8,128)} %param.5) | copy-start | bytes 11010052
  351.7 57.2 %reduce-scatter.5.cloned.1.call-start = ((), (), s32[]{:S(2)}) async-start(), calls=%async_computation.5 | async-start | bytes 655360 | tf_op jit(solution)/shard_map/reduce_scatter | solution.py:41
  384.9 67.7 %all-gather.9.cloned.1.call-start = ((), (), s32[]{:S(2)}) async-start(), calls=%async_computation.7 | async-start | bytes 2228224 | tf_op jit(solution)/shard_map/all_gather | solution.py:35
  409.0 118.2 %all-gather.11.cloned.1.call-start = ((), (), s32[]{:S(2)}) async-start(), calls=%async_computation.8 | async-start | bytes 4456448 | tf_op jit(solution)/shard_map/all_gather | solution.py:76
  529.6 2.2 copy-start.2
  531.8 2.9 copy-start.5
Sparse Core Ops, SparseCore 0:
  45.4 51.7 all-gather.6
  104.5 94.1 all-reduce.2
  351.9 33.0 reduce-scatter.2
  387.3 21.5 reduce-scatter.4
  410.6 41.9 all-gather.8
  473.1 53.9 all-gather.10
